TPU v7x, 256 devices: a whole 4x4x8 slice. The times are simulated.
256 devices in a mesh: walk: 64 (over z, x, core), elec: 2 (over y_lo), chol: 2 (over y_hi).
Axes of the slice: x: 4, y: 4 (y_hi: 2, y_lo: 2; y = y_hi * 2 + y_lo), z: 8, core: 2. Of those that a mesh axis runs over, the one named last changes fastest.
Arguments:
- green: bfloat16 [64, 1024, 256], P('walk'), may hold values from -6 to 6
- chol_vecs: bfloat16 [128, 256, 1024], P(('walk', 'chol'), 'elec'), may hold values from -0.1875 to 0.1875
Outputs:
- gradient: float32 [64, 1024, 256], P('walk', ('elec', 'chol'))
All inputs are finite; a program needn't handle non-finite values.
Results may differ from a plain program's by a relative error of at most 0.0029.
Values may be sent and summed in bfloat16 or wider, within the bound.
No kernel may reach another device: no remote copies, remote signals or barrier semaphores. Data moves between devices by JAX's collectives and lax.ppermute only.
A program may use at most 64 MiB of HBM per device.

v0:
```python
import jax
import jax.numpy as jnp
from jax import lax
from jax.sharding import PartitionSpec as P


def cut_along(value, dim, devices):
    dims = value.shape
    pieces = value.reshape(*dims[:dim], devices, dims[dim] // devices, *dims[dim + 1 :])
    return jnp.moveaxis(pieces, dim, 0)


def sent_and_summed(value, axis, dim):
    devices = lax.axis_size(axis)
    pieces = lax.all_to_all(cut_along(value, dim, devices), axis, 0, 0, tiled=True)
    return jnp.sum(pieces, axis=0)


def shards(green, chol_vecs):
    walkers, orbitals, electrons = green.shape
    starting = jnp.zeros((walkers, orbitals, electrons), jnp.float32)
    blocks = lax.all_gather(chol_vecs, "walk", axis=0, tiled=True)
    number = blocks.shape[0]
    own_rows = blocks.shape[1]
    intersection = jnp.einsum(
        "gap,wpb->gwab", blocks, green, preferred_element_type=jnp.float32
    ).astype(jnp.bfloat16)
    flattened = intersection.reshape(number * walkers, own_rows, electrons)
    received = lax.all_to_all(flattened, "elec", split_axis=2, concat_axis=1, tiled=True)
    received = received.reshape(number, walkers, electrons, own_rows)
    running = starting - jnp.einsum(
        "gap,gwba->wpb", blocks, received, preferred_element_type=jnp.float32
    )
    return sent_and_summed(running, ("elec", "chol"), 1)


def solution(mesh):
    in_specs = (P("walk", None, None), P(("walk", "chol"), "elec", None))
    out_specs = P("walk", ("elec", "chol"), None)
    return jax.shard_map(shards, mesh=mesh, in_specs=in_specs, out_specs=out_specs, check_vma=False)
```

profile of v0, /device:TPU:1, one launch (start us, length us, event | category | flops | bytes accessed | tf_op | source)
XLA Modules:
  0.0 216.9 jit_solution(13085413836040828530)
XLA Ops:
  6.5 0.0 copy-start
  6.5 0.0 all-gather.2.cloned.1.call-start
  6.5 0.7 all-gather.2.cloned.1.call-update
  7.3 106.3 %all-gather.2.cloned.1.call-done = bf16[64,128,1024]{2,1,0:T(8,128)(2,1)} async-done(((bf16[1,128,1024]{2,1,0:T(8,128)(2,1)}), bf16[64,128,1024]{2,1,0:T(8,128)(2,1)}) %all-gather.2.cloned.1.call-update) | async-done | bytes 16777232 | tf_op jit(solution)/shard_map/all_gather | solution.py:22
  113.5 0.0 copy-done
  113.5 8.2 %convert_bitcast_fusion = bf16[64,128,256]{1,2,0:T(8,128)(2,1)S(1)} fusion(bf16[64,128,1024]{2,1,0:T(8,128)(2,1)} %all-gather.2.cloned.1.call-done, bf16[1,1024,256]{2,1,0:T(8,128)(2,1)S(1)} %copy-done), kind=kOutput, calls=%fused_computation | convolution fusion | flops 4297064448 | bytes 21495808 | tf_op jit(solution)/shard_map/gap,wpb->gwab/dot_general | solution.py:25
  121.8 2.7 %copy.6 = bf16[64,128,256]{1,0,2:T(8,128)(2,1)S(1)} copy(bf16[64,128,256]{1,2,0:T(8,128)(2,1)S(1)} %convert_bitcast_fusion) | data formatting | bytes 8388608 | tf_op jit(solution)/shard_map/reshape | solution.py:28
  124.5 50.9 %all_to_all.20 = bf16[64,128,256]{1,0,2:T(8,128)(2,1)} all-to-all(bf16[64,128,256]{1,0,2:T(8,128)(2,1)S(1)} %copy.6), channel_id=1, replica_groups=mesh['walk'=64,'elec'=2,'chol'=2] {'elec'}, dimensions={2} | all-to-all | bytes 8388608 | tf_op jit(solution)/shard_map/all_to_all | solution.py:29
  175.3 6.9 %copy.7 = bf16[64,128,2,128]{3,1,2,0:T(8,128)(2,1)} copy(bf16[64,128,2,128]{1,0,3,2:T(8,128)(2,1)} %bitcast.30) | data formatting | bytes 8388608 | tf_op jit(solution)/shard_map/all_to_all | solution.py:29
  182.2 9.7 %fusion = f32[256,1024]{1,0:T(8,128)S(1)} fusion(bf16[64,256,128]{2,1,0:T(8,128)(2,1)} %bitcast.31, bf16[64,128,1024]{2,1,0:T(8,128)(2,1)} %all-gather.2.cloned.1.call-done), kind=kOutput, calls=%fused_computation.2 | convolution fusion | flops 4295229440 | bytes 22020096 | tf_op jit(solution)/shard_map/gap,gwba->wpb/dot_general | solution.py:31
  192.0 0.1 copy.16
  192.1 17.1 %all_to_all.21 = f32[4,1,256,256]{2,3,1,0:T(8,128)S(1)} all-to-all(f32[4,1,256,256]{2,3,1,0:T(8,128)S(1)} %bitcast.32), channel_id=1, replica_groups=mesh['walk'=64,'elec'=2,'chol'=2] {'elec','chol'}, dimensions={0} | all-to-all | bytes 2097152 | tf_op jit(solution)/shard_map/all_to_all | solution.py:15
  209.2 0.1 reduce_sum.11
  209.3 0.8 copy.10
Async XLA Ops:
  6.5 107.0 %copy-start = (bf16[1,1024,256]{2,1,0:T(8,128)(2,1)S(1)}, bf16[1,1024,256]{2,1,0:T(8,128)(2,1)}, u32[]{:S(2)}) copy-start(bf16[1,1024,256]{2,1,0:T(8,128)(2,1)} %param.2) | copy-start | bytes 1572868
  6.5 107.0 %all-gather.2.cloned.1.call-start = ((), (), s32[]{:S(2)}) async-start(), calls=%async_computation.2 | async-start | bytes 17039360 | tf_op jit(solution)/shard_map/all_gather | solution.py:22
Sparse Core Ops, SparseCore 0:
  10.1 103.3 all-gather.1
where the time goes:
time: 217 us
  waiting for transfers between devices  107 us (49%)
  blocking collectives  68 us (31%)
  matrix products  17.9 us (8%)
  between operations  13.4 us (6%)
  local copies, waits for them, and re-layouts  10.5 us (5%)
    all_gather x1, waiting for transfers between devices, shards(): blocks = lax.all_gather(chol_vecs, 'walk', axis=0, tiled=True)  106 us
    all_to_all x1, blocking collectives, shards(): lax.all_to_all(flattened, 'elec', split_axis=2, concat_axis=1, tiled=True)  50.9 us
    all_to_all x1, blocking collectives, sent_and_summed(): lax.all_to_all(cut_along(value, dim, devices), axis, 0, 0, tiled=True)  17.1 us
    dot_general x1, matrix products, shards(): jnp.einsum('gap,gwba->wpb', blocks, received, preferred_element_type=jnp....  9.74 us
    dot_general x1, matrix products, shards(): jnp.einsum('gap,wpb->gwab', blocks, green, preferred_element_type=jnp.flo...  8.21 us
    all_to_all x1, local copies, waits for them, and re-layouts, shards(): lax.all_to_all(flattened, 'elec', split_axis=2, concat_axis=1, tiled=True)  6.87 us
  transfers between devices with their start and end apart: 1, of which 1 were waited for; matrix products, arithmetic and copies ran while one was open for 0% of the time, Pallas kernels for 0%

commit v1 on v0

--- a/solution.py
+++ b/solution.py
@@ -19,7 +19,9 @@
 def shards(green, chol_vecs):
     walkers, orbitals, electrons = green.shape
     starting = jnp.zeros((walkers, orbitals, electrons), jnp.float32)
-    blocks = lax.all_gather(chol_vecs, "walk", axis=0, tiled=True)
+    blocks = jnp.concatenate(
+        lax.all_to_all(jnp.stack([chol_vecs] * lax.axis_size("walk")), "walk", 0, 0), axis=0
+    )
     number = blocks.shape[0]
     own_rows = blocks.shape[1]
     intersection = jnp.einsum(

time: 217 us -> 479 us (2.21); the launches traced: 217 us -> 474 us
  blocking collectives: 68 us -> 442 us
  waiting for transfers between devices: 107 us -> 0 us
  between operations: 13.4 us -> 0.05 us
    all_to_all x0 -> x1, blocking collectives: none -> 377 us  [shards(): lax.all_to_all(jnp.stack([chol_vecs] * lax.axis_size('walk')), 'walk', 0, 0)]
    all_gather x1 -> x0, waiting for transfers between devices: 106 us -> none  [shards(): blocks = lax.all_gather(chol_vecs, 'walk', axis=0, tiled=True)]
  transfers between devices with their start and end apart: 1 -> 0, of which waited for: 1 -> 0; matrix products, arithmetic and copies ran while one was open for 0% -> 0% of each run, Pallas kernels for 0% -> 0%
where the time goes in v1:
time: 479 us; the launch traced here: 474 us
  blocking collectives  442 us (92%)
  matrix products  17.9 us (4%)
  local copies, waits for them, and re-layouts  13.9 us (3%)
    all_to_all x1, blocking collectives, shards(): lax.all_to_all(jnp.stack([chol_vecs] * lax.axis_size('walk')), 'walk', 0, 0)  377 us
    all_to_all x1, blocking collectives, shards(): lax.all_to_all(flattened, 'elec', split_axis=2, concat_axis=1, tiled=True)  49.1 us
    all_to_all x1, blocking collectives, sent_and_summed(): lax.all_to_all(cut_along(value, dim, devices), axis, 0, 0, tiled=True)  15.7 us
    dot_general x1, matrix products, shards(): jnp.einsum('gap,gwba->wpb', blocks, received, preferred_element_type=jnp....  9.74 us

profile of v1, /device:TPU:1, one launch (start us, length us, event | category | flops | bytes accessed | tf_op | source)
XLA Modules:
  0.0 473.9 jit_solution(12670595391196287009)
XLA Ops:
  0.0 0.0 copy-start
  0.0 3.4 stack.2
  3.4 377.2 %all_to_all.25 = bf16[64,1,128,1024]{3,2,1,0:T(8,128)(2,1)} all-to-all(bf16[64,1,128,1024]{3,2,1,0:T(8,128)(2,1)S(1)} %stack.2), channel_id=1, replica_groups=mesh['walk'=64,'elec'=2,'chol'=2] {'walk'}, dimensions={0} | all-to-all | bytes 33554432 | tf_op jit(solution)/shard_map/all_to_all | solution.py:23
  380.6 0.0 copy-done
  380.6 8.2 %convert_bitcast_fusion = bf16[64,128,256]{1,2,0:T(8,128)(2,1)S(1)} fusion(bf16[64,1,128,1024]{3,2,1,0:T(8,128)(2,1)} %all_to_all.25, bf16[1,1024,256]{2,1,0:T(8,128)(2,1)S(1)} %copy-done), kind=kOutput, calls=%fused_computation.4 | convolution fusion | flops 4297064448 | bytes 21495808 | tf_op jit(solution)/shard_map/gap,wpb->gwab/dot_general | solution.py:27
  388.8 2.7 copy.6
  391.5 49.1 %all_to_all.26 = bf16[64,128,256]{1,0,2:T(8,128)(2,1)} all-to-all(bf16[64,128,256]{1,0,2:T(8,128)(2,1)S(1)} %copy.6), channel_id=1, replica_groups=mesh['walk'=64,'elec'=2,'chol'=2] {'elec'}, dimensions={2} | all-to-all | bytes 8388608 | tf_op jit(solution)/shard_map/all_to_all | solution.py:31
  440.6 6.9 %copy.7 = bf16[64,128,2,128]{3,1,2,0:T(8,128)(2,1)} copy(bf16[64,128,2,128]{1,0,3,2:T(8,128)(2,1)} %bitcast.40) | data formatting | bytes 8388608 | tf_op jit(solution)/shard_map/all_to_all | solution.py:31
  447.5 9.7 %fusion.9 = f32[256,1024]{1,0:T(8,128)S(1)} fusion(bf16[64,256,128]{2,1,0:T(8,128)(2,1)} %bitcast.41, bf16[64,1,128,1024]{3,2,1,0:T(8,128)(2,1)} %all_to_all.25), kind=kOutput, calls=%fused_computation.6 | convolution fusion | flops 4295229440 | bytes 22020096 | tf_op jit(solution)/shard_map/gap,gwba->wpb/dot_general | solution.py:33
  457.2 0.1 copy.16
  457.3 15.7 %all_to_all.27 = f32[4,1,256,256]{2,3,1,0:T(8,128)S(1)} all-to-all(f32[4,1,256,256]{2,3,1,0:T(8,128)S(1)} %bitcast.42), channel_id=1, replica_groups=mesh['walk'=64,'elec'=2,'chol'=2] {'elec','chol'}, dimensions={0} | all-to-all | bytes 2097152 | tf_op jit(solution)/shard_map/all_to_all | solution.py:15
  473.0 0.1 reduce_sum.11
  473.1 0.8 copy.10
Async XLA Ops:
  0.0 380.6 %copy-start = (bf16[1,1024,256]{2,1,0:T(8,128)(2,1)S(1)}, bf16[1,1024,256]{2,1,0:T(8,128)(2,1)}, u32[]{:S(2)}) copy-start(bf16[1,1024,256]{2,1,0:T(8,128)(2,1)} %param.2) | copy-start | bytes 1572868
